TPU v7x, 32 devices: a whole 2x2x4 slice. The times are simulated.
32 devices in a mesh: col: 2 (over core), dev: 16 (over z, y, x).
Axes of the slice: x: 2, y: 2, z: 4, core: 2. Of those that a mesh axis runs over, the one named last changes fastest.
Arguments:
- factor_a: float32 [1536, 16, 512], P('dev'), may hold values from -1 to 1
- factor_b: float32 [1536, 64, 512], P('dev', 'col'), may hold values from -1 to 1
- factor_occ: float32 [1536, 16, 512], P('dev'), may hold values from -1 to 1
- singles_a: float32 [16, 16], replicated, may hold values from -1.5 to 1.5
- singles_b: float32 [16, 64], P(None, 'col'), may hold values from -1.5 to 1.5
- doubles: bfloat16 [512, 512, 256], P('col', 'dev'), may hold values from -0.023925781 to 0.023925781
- orbital_a: float32 [16], P('col'), may hold values from 0.2 to 3
- orbital_b: float32 [64], P('dev'), may hold values from 0.2 to 3
- orbital_occ: float32 [16], replicated, may hold values from -2 to -0.3
Outputs:
- update: float32 [16, 64, 256], P('col', 'dev')
All inputs are finite; a program needn't handle non-finite values.
Results may differ from a plain program's by a relative error of at most 0.0049.
Values may be sent and summed in bfloat16 or wider, within the bound.
No kernel may reach another device: no remote copies, remote signals or barrier semaphores. Data moves between devices by JAX's collectives and lax.ppermute only.
A program may use at most 128 MiB of HBM per device.

v0:
```python
import jax
import jax.numpy as jnp
from jax import lax
from jax.sharding import PartitionSpec as P


def body(
    factor_a, factor_b, factor_occ, singles_a, singles_b, doubles, orbital_a, orbital_b, orbital_occ
):
    highest = lax.Precision.HIGHEST
    c_tile = doubles.shape[0]
    d_tile = doubles.shape[1]
    pair_count = doubles.shape[2]
    shard_rows = factor_a.shape[0]
    a_rows = factor_a.shape[1]
    b_local = factor_b.shape[1]
    d_groups = factor_b.shape[2] // d_tile
    col_index = lax.axis_index("col")
    occ_tile = lax.dynamic_slice_in_dim(factor_occ, col_index * c_tile, c_tile, 2)
    a_tile = lax.dynamic_slice_in_dim(factor_a, col_index * c_tile, c_tile, 2)
    dressed_a = (a_tile - jnp.einsum("ka,qkc->qac", singles_a, occ_tile, precision=highest)).astype(
        jnp.bfloat16
    )
    dressed_a = dressed_a.reshape(shard_rows, a_rows * c_tile)
    dressed_b = (
        factor_b - jnp.einsum("kb,qkd->qbd", singles_b, factor_occ, precision=highest)
    ).astype(jnp.bfloat16)
    grouped = dressed_b.reshape(shard_rows, b_local, d_groups, d_tile)
    grouped = jnp.transpose(grouped, (0, 2, 1, 3)).reshape(shard_rows, d_groups, b_local * d_tile)
    moved = lax.all_to_all(grouped, "dev", split_axis=1, concat_axis=0, tiled=True)
    collected = lax.all_gather(moved, "col", axis=1, tiled=True)
    whole_b = collected.reshape(collected.shape[0], -1)
    b_rows_all = whole_b.shape[1] // d_tile
    contract_first = (((0,), (0,)), ((), ()))
    whole_a = lax.all_gather(dressed_a, "dev", axis=0, tiled=True)
    integral = lax.dot_general(whole_a, whole_b, contract_first, preferred_element_type=jnp.float32)
    integral = integral.astype(jnp.bfloat16).reshape(a_rows, c_tile, b_rows_all, d_tile)
    integral = jnp.transpose(integral, (0, 2, 1, 3)).reshape(a_rows * b_rows_all, c_tile * d_tile)
    partial_value = jnp.dot(
        integral, doubles.reshape(c_tile * d_tile, pair_count), preferred_element_type=jnp.float32
    )
    partial_value = partial_value.reshape(a_rows, b_rows_all, pair_count)
    reduced = lax.psum_scatter(partial_value, "dev", scatter_dimension=1, tiled=True)
    total = lax.psum_scatter(reduced, "col", scatter_dimension=0, tiled=True)
    pair_energy = (orbital_occ[:, None] + orbital_occ[None, :]).reshape(-1)
    denominator = orbital_a[:, None, None] + orbital_b[None, :, None] - pair_energy[None, None, :]
    return total / denominator


def solution(mesh):
    return jax.shard_map(
        body,
        mesh=mesh,
        in_specs=(
            P("dev", None, None),
            P("dev", "col", None),
            P("dev", None, None),
            P(),
            P(None, "col"),
            P("col", "dev", None),
            P("col"),
            P("dev"),
            P(),
        ),
        out_specs=P("col", "dev", None),
        check_vma=False,
    )
```

profile of v0, /device:TPU:0, one launch (start us, length us, event | category | flops | bytes accessed | tf_op | source)
XLA Modules:
  0.0 448.8 jit_solution(5826299409805732357)
XLA Ops:
  6.5 1.9 copy-done
  8.4 8.8 %fusion.2 = bf16[96,32,512]{2,1,0:T(8,128)(2,1)} fusion(f32[96,32,512]{2,1,0:T(8,128)} %param.10, f32[96,16,512]{2,1,0:T(8,128)S(1)} %copy-done, f32[16,32]{1,0:T(8,128)} %param.13), kind=kOutput, calls=%fused_computation.4 | convolution fusion | flops 305135616 | bytes 12584960 | tf_op jit(solution)/shard_map/kb,qkd->qbd/dot_general | solution.py:26
  17.2 7.4 %copy.29 = bf16[96,32,512]{0,2,1:T(8,128)(2,1)} copy(bf16[96,32,512]{2,1,0:T(8,128)(2,1)} %fusion.2) | data formatting | bytes 6291456 | tf_op jit(solution)/shard_map/convert_element_type | solution.py:27
  24.6 5.3 %copy.30 = bf16[96,16,32,32]{0,3,2,1:T(8,128)(2,1)} copy(bf16[96,16,32,32]{0,3,1,2:T(8,128)(2,1)} %bitcast.48) | data formatting | bytes 6291456 | tf_op jit(solution)/shard_map/transpose | solution.py:29
  29.8 6.0 %copy.31 = bf16[96,16,1024]{2,0,1:T(8,128)(2,1)} copy(bf16[96,16,1024]{0,2,1:T(8,128)(2,1)} %bitcast.49) | data formatting | bytes 6291456 | tf_op jit(solution)/shard_map/reshape | solution.py:29
  35.9 79.8 %all_to_all.18 = bf16[96,16,1024]{2,0,1:T(8,128)(2,1)} all-to-all(bf16[96,16,1024]{2,0,1:T(8,128)(2,1)} %copy.31), channel_id=1, replica_groups=mesh['col'=2,'dev'=16] {'dev'}, dimensions={1} | all-to-all | bytes 6291456 | tf_op jit(solution)/shard_map/all_to_all | solution.py:30
  115.7 0.0 all-gather.5.cloned.1.call-update
  115.7 0.0 all-gather.3.cloned.1.call-start
  115.8 2.9 fusion.5
  118.7 1.2 copy.39
  119.9 0.0 all-gather.3.cloned.1.call-update
  119.9 0.2 reduce-scatter.3.cloned.1.call-start
  120.2 10.8 %all-gather.5.cloned.1.call-done = bf16[1536,2,1024]{2,0,1:T(8,128)(2,1)} async-done(((bf16[1536,1,1024]{2,0,1:T(8,128)(2,1)}), bf16[1536,2,1024]{2,0,1:T(8,128)(2,1)}) %all-gather.5.cloned.1.call-update) | async-done | bytes 6291472 | tf_op jit(solution)/shard_map/all_gather | solution.py:31
  131.0 8.7 %copy.32 = bf16[1536,2,1024]{0,2,1:T(8,128)(2,1)} copy(bf16[1536,2,1024]{2,0,1:T(8,128)(2,1)} %all-gather.5.cloned.1.call-done) | data formatting | bytes 12582912 | tf_op jit(solution)/shard_map/all_gather | solution.py:31
  139.6 146.7 %all-gather.3.cloned.1.call-done = bf16[1536,4096]{1,0:T(8,128)(2,1)} async-done(((bf16[96,4096]{1,0:T(8,128)(2,1)}), bf16[1536,4096]{1,0:T(8,128)(2,1)}) %all-gather.3.cloned.1.call-update) | async-done | bytes 12582928 | tf_op jit(solution)/shard_map/all_gather | solution.py:35
  286.4 32.6 %convolution_convert_fusion = bf16[4096,2048]{1,0:T(8,128)(2,1)} fusion(bf16[1536,4096]{1,0:T(8,128)(2,1)} %all-gather.3.cloned.1.call-done, bf16[1536,2048]{0,1:T(8,128)(2,1)} %bitcast.52), kind=kOutput, calls=%fused_computation.2 | convolution fusion | flops 25778192384 | bytes 35651584 | tf_op jit(solution)/shard_map/dot_general | solution.py:36
  318.9 21.4 %copy.33 = bf16[4096,2048]{0,1:T(8,128)(2,1)} copy(bf16[4096,2048]{1,0:T(8,128)(2,1)} %convolution_convert_fusion) | data formatting | bytes 33554432 | tf_op jit(solution)/shard_map/convert_element_type | solution.py:37
  340.3 10.7 %copy.40 = bf16[256,8,16,256]{3,2,1,0:T(8,128)(2,1)S(1)} copy(bf16[256,8,16,256]{3,1,2,0:T(8,128)(2,1)} %bitcast.47) | data formatting | bytes 33554432
  351.0 0.0 copy-start.3
  351.0 0.0 copy-start.4
  351.1 0.0 copy-start.1
  351.1 6.7 %fusion.10 = f32[16,64,256]{2,0,1:T(8,128)} fusion(bf16[256,32,256]{2,1,0:T(8,128)(2,1)S(1)} %copy-done.6, bf16[16,256,64,32]{1,0,3,2:T(8,128)(2,1)S(1)} %bitcast.50), kind=kOutput, calls=%fused_computation.11 | convolution fusion | flops 4294967296 | bytes 22020096 | tf_op jit(solution)/shard_map/dot_general | solution.py:39
  357.8 0.0 reduce-scatter.3.cloned.1.call-update
  357.8 0.0 reduce-scatter.5.cloned.1.call-start
  357.9 0.1 broadcast_add_fusion
  358.0 0.1 add.53
  358.0 76.8 %reduce-scatter.3.cloned.1.call-done = f32[16,4,256]{2,0,1:T(8,128)} async-done(((f32[16,64,256]{2,0,1:T(8,128)}), f32[16,4,256]{2,0,1:T(8,128)}) %reduce-scatter.3.cloned.1.call-update) | async-done | bytes 65552 | tf_op jit(solution)/shard_map/reduce_scatter | solution.py:43
  434.9 0.0 reduce-scatter.5.cloned.1.call-update
  434.9 0.1 broadcast_add_fusion.1
  435.0 5.8 %reduce-scatter.5.cloned.1.call-done = f32[8,4,256]{2,0,1:T(8,128)} async-done(((f32[16,4,256]{2,0,1:T(8,128)}), f32[8,4,256]{2,0,1:T(8,128)}) %reduce-scatter.5.cloned.1.call-update) | async-done | bytes 32784 | tf_op jit(solution)/shard_map/reduce_scatter | solution.py:44
  440.8 0.8 subtract_divide_fusion
  441.6 0.6 copy.35
  (11 shorter events, 0.0 us)
Async XLA Ops:
  6.5 1.9 copy-start
  6.5 124.4 %all-gather.5.cloned.1.call-start = ((), (), s32[]{:S(2)}) async-start(), calls=%async_computation.4 | async-start | bytes 9437184 | tf_op jit(solution)/shard_map/all_gather | solution.py:31
  35.9 79.9 %copy-start.2 = (f32[16,16]{1,0:T(8,128)S(1)}, f32[16,16]{1,0:T(8,128)}, u32[]{:S(2)}) copy-start(f32[16,16]{1,0:T(8,128)} %param.12) | copy-start | bytes 3076
  115.7 170.6 %all-gather.3.cloned.1.call-start = ((), (), s32[]{:S(2)}) async-start(), calls=%async_computation.3 | async-start | bytes 13369344 | tf_op jit(solution)/shard_map/all_gather | solution.py:35
  119.9 314.9 %reduce-scatter.3.cloned.1.call-start = ((), (), s32[]{:S(2)}) async-start(), calls=%async_computation.5 | async-start | bytes 1114112 | tf_op jit(solution)/shard_map/reduce_scatter | solution.py:43
  340.3 10.7 %copy-start.6 = (bf16[256,32,256]{2,1,0:T(8,128)(2,1)S(1)}, bf16[256,32,256]{2,1,0:T(8,128)(2,1)}, u32[]{:S(2)}) copy-start(bf16[256,32,256]{2,1,0:T(8,128)(2,1)} %param.14) | copy-start | bytes 12582916
  351.0 6.8 %copy-start.3 = (f32[16]{0:T(128)S(1)}, f32[16]{0:T(128)}, u32[]{:S(2)}) copy-start(f32[16]{0:T(128)} %param.17) | copy-start | bytes 196
  351.0 83.8 %copy-start.4 = (f32[4]{0:T(128)S(1)}, f32[4]{0:T(128)}, u32[]{:S(2)}) copy-start(f32[4]{0:T(128)} %param.16) | copy-start | bytes 52
  351.1 83.8 %copy-start.5 = (f32[8]{0:T(128)S(1)}, f32[8]{0:T(128)}, u32[]{:S(2)}) copy-start(f32[8]{0:T(128)} %param.15) | copy-start | bytes 100
  351.1 91.2 %copy-start.1 = (f32[96,16,512]{2,1,0:T(8,128)S(1)}, f32[96,16,512]{2,1,0:T(8,128)}, u32[]{:S(2)}) copy-start(f32[96,16,512]{2,1,0:T(8,128)} %param.11) | copy-start | bytes 9437188
  357.8 83.0 %reduce-scatter.5.cloned.1.call-start = ((), (), s32[]{:S(2)}) async-start(), calls=%async_computation.6 | async-start | bytes 98304 | tf_op jit(solution)/shard_map/reduce_scatter | solution.py:44
Sparse Core Ops, SparseCore 0:
  115.8 15.0 all-gather.4
  133.7 152.5 all-gather.2
  357.9 76.8 reduce-scatter.2
  436.9 3.8 reduce-scatter.4
where the time goes:
time: 450 us; the launch traced here: 449 us
  waiting for transfers between devices  240 us (53%)
  blocking collectives  79.8 us (18%)
  local copies, waits for them, and re-layouts  63.3 us (14%)
  matrix products  51 us (11%)
  between operations  13.2 us (3%)
    all_gather x1, waiting for transfers between devices, body(): whole_a = lax.all_gather(dressed_a, 'dev', axis=0, tiled=True)  147 us
    all_to_all x1, blocking collectives, body(): lax.all_to_all(grouped, 'dev', split_axis=1, concat_axis=0, tiled=True)  79.8 us
    reduce_scatter x1, waiting for transfers between devices, body(): lax.psum_scatter(partial_value, 'dev', scatter_dimension=1, tiled=True)  76.8 us
    dot_general x1, matrix products, body(): lax.dot_general(whole_a, whole_b, contract_first, preferred_element_type=...  32.6 us
    convert_element_type x1, local copies, waits for them, and re-layouts, body(): integral.astype(jnp.bfloat16).reshape(a_rows, c_tile, b_rows_all, d_tile)  21.4 us
    unnamed x16, local copies, waits for them, and re-layouts  13.8 us
    all_gather x1, waiting for transfers between devices, body(): collected = lax.all_gather(moved, 'col', axis=1, tiled=True)  10.8 us
  transfers between devices with their start and end apart: 4, of which 4 were waited for; matrix products, arithmetic and copies ran while one was open for 3% of the time, Pallas kernels for 0%

commit v1 on v0

--- a/solution.py
+++ b/solution.py
@@ -2,6 +2,27 @@
 import jax.numpy as jnp
 from jax import lax
 from jax.sharding import PartitionSpec as P
+from jax.lax import axis_index, axis_size, ppermute
+
+
+def play_rates_on(s0, lane_axis):
+    axis_len = axis_size(lane_axis)
+    table = []
+    for j in tuple(range(axis_len)):
+        table.append((j, (j + 1) % axis_len))
+    pages = []
+    for j in tuple(range(axis_len)):
+        pages.append((j, (j - 1) % axis_len))
+    back, spare = ([s0], [s0])
+    for _ in range(axis_len // 2):
+        t1 = ppermute(back[-1], axis_name=lane_axis, perm=table)
+        back.append(t1)
+    for _ in [*range((axis_len - 1) // 2)]:
+        high = ppermute(spare[-1], perm=pages, axis_name=lane_axis)
+        spare.append(high)
+    front = jnp.concatenate([*back[::-1], *spare[1:]], 0)
+    fresh = axis_index(lane_axis)
+    return jnp.roll(front, shift=(fresh - axis_len // 2) * s0.shape[0], axis=0)
 
 
 def body(
@@ -32,7 +53,7 @@
     whole_b = collected.reshape(collected.shape[0], -1)
     b_rows_all = whole_b.shape[1] // d_tile
     contract_first = (((0,), (0,)), ((), ()))
-    whole_a = lax.all_gather(dressed_a, "dev", axis=0, tiled=True)
+    whole_a = play_rates_on(dressed_a, "dev")
     integral = lax.dot_general(whole_a, whole_b, contract_first, preferred_element_type=jnp.float32)
     integral = integral.astype(jnp.bfloat16).reshape(a_rows, c_tile, b_rows_all, d_tile)
     integral = jnp.transpose(integral, (0, 2, 1, 3)).reshape(a_rows * b_rows_all, c_tile * d_tile)

time: 450 us -> 579 us (1.29)
  blocking collectives: 79.8 us -> 0 us
  waiting for transfers between devices: 240 us -> 319 us
  starting transfers between devices: 0.31 us -> 67.1 us
  local copies, waits for them, and re-layouts: 63.3 us -> 125 us
    ppermute x0 -> x15, waiting for transfers between devices: none -> 210 us  [the longest x8 144 us: play_rates_on(): t1 = ppermute(back[-1], axis_name=lane_axis, perm=table)]
    all_gather x1 -> x0, waiting for transfers between devices: 147 us -> none  [body(): whole_a = lax.all_gather(dressed_a, 'dev', axis=0, tiled=True)]
    all_to_all x1 -> x0, blocking collectives: 79.8 us -> none  [body(): lax.all_to_all(grouped, 'dev', split_axis=1, concat_axis=0, tiled=True)]
    ppermute x0 -> x15, starting transfers between devices: none -> 60.9 us  [the longest x8 51.9 us: play_rates_on(): t1 = ppermute(back[-1], axis_name=lane_axis, perm=table)]
    unnamed x16 -> x83, local copies, waits for them, and re-layouts: 13.8 us -> 73.8 us
    reduce_scatter x1, waiting for transfers between devices: 76.8 us -> 102 us  [body(): lax.psum_scatter(partial_value, 'dev', scatter_dimension=1, tiled=True)]
    all_gather x1, waiting for transfers between devices: 10.8 us -> 0.01 us  [body(): collected = lax.all_gather(moved, 'col', axis=1, tiled=True)]
    all_to_all x0 -> x1, starting transfers between devices: none -> 5.94 us  [body(): lax.all_to_all(grouped, 'dev', split_axis=1, concat_axis=0, tiled=True)]
  transfers between devices with their start and end apart: 4 -> 19, of which waited for: 4 -> 14; matrix products, arithmetic and copies ran while one was open for 3% -> 15% of each run, Pallas kernels for 0% -> 0%
where the time goes in v1:
time: 579 us; the launch traced here: 576 us
  waiting for transfers between devices  319 us (55%)
  local copies, waits for them, and re-layouts  125 us (22%)
  starting transfers between devices  67.1 us (12%)
  matrix products  51.1 us (9%)
  between operations  13.4 us (2%)
    ppermute x8, waiting for transfers between devices, play_rates_on(): t1 = ppermute(back[-1], axis_name=lane_axis, perm=table)  144 us
    reduce_scatter x1, waiting for transfers between devices, body(): lax.psum_scatter(partial_value, 'dev', scatter_dimension=1, tiled=True)  102 us
    unnamed x83, local copies, waits for them, and re-layouts  73.8 us
    ppermute x7, waiting for transfers between devices, play_rates_on(): high = ppermute(spare[-1], perm=pages, axis_name=lane_axis)  65.9 us
    ppermute x8, starting transfers between devices, play_rates_on(): t1 = ppermute(back[-1], axis_name=lane_axis, perm=table)  51.9 us
    dot_general x1, matrix products, body(): lax.dot_general(whole_a, whole_b, contract_first, preferred_element_type=...  32.7 us
    convert_element_type x1, local copies, waits for them, and re-layouts, body(): integral.astype(jnp.bfloat16).reshape(a_rows, c_tile, b_rows_all, d_tile)  20.7 us
  transfers between devices with their start and end apart: 19, of which 14 were waited for; matrix products, arithmetic and copies ran while one was open for 15% of the time, Pallas kernels for 0%

profile of v1, /device:TPU:0, one launch (start us, length us, event | category | flops | bytes accessed | tf_op | source)
XLA Modules:
  0.0 576.3 jit_solution(8490889482776840341)
XLA Ops:
  8.4 2.9 fusion.6
  12.6 3.0 collective-permute-start
  15.5 8.8 %fusion.3 = bf16[96,32,512]{2,1,0:T(8,128)(2,1)} fusion(f32[96,32,512]{2,1,0:T(8,128)} %param.10, f32[96,16,512]{2,1,0:T(8,128)S(1)} %copy-done, f32[16,32]{1,0:T(8,128)} %param.13), kind=kOutput, calls=%fused_computation.5 | convolution fusion | flops 305135616 | bytes 12584960 | tf_op jit(solution)/shard_map/kb,qkd->qbd/dot_general | solution.py:47
  24.3 7.4 %copy.29 = bf16[96,32,512]{0,2,1:T(8,128)(2,1)} copy(bf16[96,32,512]{2,1,0:T(8,128)(2,1)} %fusion.3) | data formatting | bytes 6291456 | tf_op jit(solution)/shard_map/convert_element_type | solution.py:48
  31.7 5.3 copy.30
  37.0 6.0 %copy.31 = bf16[96,16,1024]{2,0,1:T(8,128)(2,1)} copy(bf16[96,16,1024]{0,2,1:T(8,128)(2,1)} %bitcast.48) | data formatting | bytes 6291456 | tf_op jit(solution)/shard_map/reshape | solution.py:50
  43.0 5.9 %all-to-all-start = ((bf16[96,16,1024]{2,0,1:T(8,128)(2,1)}), bf16[96,16,1024]{2,0,1:T(8,128)(2,1)S(1)}, u32[]{:S(2)}, u32[]{:S(2)}) async-start(bf16[96,16,1024]{2,0,1:T(8,128)(2,1)} %copy.31), calls=%async_computation | async-start | bytes 6291456 | tf_op jit(solution)/shard_map/all_to_all | solution.py:51
  51.0 3.7 collective-permute-start.8
  54.7 68.8 %collective-permute-done.1 = bf16[96,4096]{1,0:T(8,128)(2,1)S(1)} collective-permute-done((bf16[96,4096]{1,0:T(8,128)(2,1)}, bf16[96,4096]{1,0:T(8,128)(2,1)S(1)}, u32[]{:S(2)}, u32[]{:S(2)}) %collective-permute-start.1) | collective-permute-done | bytes 786464 | tf_op jit(solution)/shard_map/ppermute | solution.py:18
  123.5 2.8 collective-permute-done.8
  127.2 2.9 collective-permute-start.9
  130.1 26.0 %collective-permute-done.2 = bf16[96,4096]{1,0:T(8,128)(2,1)S(1)} collective-permute-done((bf16[96,4096]{1,0:T(8,128)(2,1)S(1)}, bf16[96,4096]{1,0:T(8,128)(2,1)S(1)}, u32[]{:S(2)}, u32[]{:S(2)}) %collective-permute-start.2) | collective-permute-done | bytes 786464 | tf_op jit(solution)/shard_map/ppermute | solution.py:18
  156.1 2.5 collective-permute-start.3
  159.4 2.4 collective-permute-start.10
  161.8 15.3 %collective-permute-done.3 = bf16[96,4096]{1,0:T(8,128)(2,1)S(1)} collective-permute-done((bf16[96,4096]{1,0:T(8,128)(2,1)S(1)}, bf16[96,4096]{1,0:T(8,128)(2,1)S(1)}, u32[]{:S(2)}, u32[]{:S(2)}) %collective-permute-start.3) | collective-permute-done | bytes 786464 | tf_op jit(solution)/shard_map/ppermute | solution.py:18
  177.1 14.9 %collective-permute-done.10 = bf16[96,4096]{1,0:T(8,128)(2,1)S(1)} collective-permute-done((bf16[96,4096]{1,0:T(8,128)(2,1)S(1)}, bf16[96,4096]{1,0:T(8,128)(2,1)S(1)}, u32[]{:S(2)}, u32[]{:S(2)}) %collective-permute-start.10) | collective-permute-done | bytes 786464 | tf_op jit(solution)/shard_map/ppermute | solution.py:21
  193.0 4.2 collective-permute-done.4
  197.2 22.0 %collective-permute-start.5 = (bf16[96,4096]{1,0:T(8,128)(2,1)S(1)}, bf16[96,4096]{1,0:T(8,128)(2,1)S(1)}, u32[]{:S(2)}, u32[]{:S(2)}) collective-permute-start(bf16[96,4096]{1,0:T(8,128)(2,1)S(1)} %collective-permute-done.4), channel_id=1, source_target_pairs={{0,1},{1,2},{2,3},{3,4},{4,5},{5,6},{6,7},{7,8},{8,9},{9,10},{10,1... | collective-permute-start | bytes 2359304 | tf_op jit(solution)/shard_map/ppermute | solution.py:18
  219.2 15.9 %collective-permute-done.11 = bf16[96,4096]{1,0:T(8,128)(2,1)S(1)} collective-permute-done((bf16[96,4096]{1,0:T(8,128)(2,1)S(1)}, bf16[96,4096]{1,0:T(8,128)(2,1)S(1)}, u32[]{:S(2)}, u32[]{:S(2)}) %collective-permute-start.11) | collective-permute-done | bytes 786464 | tf_op jit(solution)/shard_map/ppermute | solution.py:21
  235.9 15.9 %collective-permute-done.5 = bf16[96,4096]{1,0:T(8,128)(2,1)S(1)} collective-permute-done((bf16[96,4096]{1,0:T(8,128)(2,1)S(1)}, bf16[96,4096]{1,0:T(8,128)(2,1)S(1)}, u32[]{:S(2)}, u32[]{:S(2)}) %collective-permute-start.5) | collective-permute-done | bytes 786464 | tf_op jit(solution)/shard_map/ppermute | solution.py:18
  251.7 2.7 collective-permute-start.6
  254.4 16.5 %collective-permute-done.12 = bf16[96,4096]{1,0:T(8,128)(2,1)} collective-permute-done((bf16[96,4096]{1,0:T(8,128)(2,1)S(1)}, bf16[96,4096]{1,0:T(8,128)(2,1)}, u32[]{:S(2)}, u32[]{:S(2)}) %collective-permute-start.12) | collective-permute-done | bytes 786464 | tf_op jit(solution)/shard_map/ppermute | solution.py:21
  271.0 19.9 %collective-permute-start.7 = (bf16[96,4096]{1,0:T(8,128)(2,1)}, bf16[96,4096]{1,0:T(8,128)(2,1)}, u32[]{:S(2)}, u32[]{:S(2)}) collective-permute-start(bf16[96,4096]{1,0:T(8,128)(2,1)} %collective-permute-done.6), channel_id=1, source_target_pairs={{0,1},{1,2},{2,3},{3,4},{4,5},{5,6},{6,7},{7,8},{8,9},{9,10},{10,1... | collective-permute-start | bytes 2359304 | tf_op jit(solution)/shard_map/ppermute | solution.py:18
  290.9 15.0 %collective-permute-done.13 = bf16[96,4096]{1,0:T(8,128)(2,1)} collective-permute-done((bf16[96,4096]{1,0:T(8,128)(2,1)}, bf16[96,4096]{1,0:T(8,128)(2,1)}, u32[]{:S(2)}, u32[]{:S(2)}) %collective-permute-start.13) | collective-permute-done | bytes 786464 | tf_op jit(solution)/shard_map/ppermute | solution.py:21
  307.9 14.2 %collective-permute-done.7 = bf16[96,4096]{1,0:T(8,128)(2,1)} collective-permute-done((bf16[96,4096]{1,0:T(8,128)(2,1)}, bf16[96,4096]{1,0:T(8,128)(2,1)}, u32[]{:S(2)}, u32[]{:S(2)}) %collective-permute-start.7) | collective-permute-done | bytes 786464 | tf_op jit(solution)/shard_map/ppermute | solution.py:18
  378.9 8.6 %copy.32 = bf16[1536,2,1024]{0,2,1:T(8,128)(2,1)} copy(bf16[1536,2,1024]{2,0,1:T(8,128)(2,1)} %all-gather.2.cloned.1.call-done) | data formatting | bytes 12582912 | tf_op jit(solution)/shard_map/all_gather | solution.py:52
  387.6 32.7 %convolution_convert_fusion = bf16[4096,2048]{1,0:T(8,128)(2,1)} fusion(bf16[1536,2048]{0,1:T(8,128)(2,1)} %bitcast.51, bf16[3072,4096]{1,0:T(8,128)(2,1)} %constant_dynamic-update-slice_fusion, s32[]{:T(128)S(6)} %select_n.19), kind=kOutput, calls=%fused_computation.2 | convolution fusion | flops 25778192384 | bytes 35651588 | tf_op jit(solution)/shard_map/dot_general | solution.py:57
  420.2 20.7 %copy.33 = bf16[4096,2048]{0,1:T(8,128)(2,1)} copy(bf16[4096,2048]{1,0:T(8,128)(2,1)} %convolution_convert_fusion) | data formatting | bytes 33554432 | tf_op jit(solution)/shard_map/convert_element_type | solution.py:58
  441.0 11.6 %copy.40 = bf16[256,8,16,256]{3,2,1,0:T(8,128)(2,1)S(1)} copy(bf16[256,8,16,256]{3,1,2,0:T(8,128)(2,1)} %bitcast.46) | data formatting | bytes 33554432
  452.6 6.7 %fusion.11 = f32[16,64,256]{2,0,1:T(8,128)} fusion(bf16[256,32,256]{2,1,0:T(8,128)(2,1)S(1)} %copy-done.24, bf16[16,256,64,32]{1,0,3,2:T(8,128)(2,1)S(1)} %bitcast.49), kind=kOutput, calls=%fused_computation.12 | convolution fusion | flops 4294967296 | bytes 22020096 | tf_op jit(solution)/shard_map/dot_general | solution.py:60
  459.6 102.4 %reduce-scatter.3.cloned.1.call-done = f32[16,4,256]{2,0,1:T(8,128)} async-done(((f32[16,64,256]{2,0,1:T(8,128)}), f32[16,4,256]{2,0,1:T(8,128)}) %reduce-scatter.3.cloned.1.call-update) | async-done | bytes 65552 | tf_op jit(solution)/shard_map/reduce_scatter | solution.py:64
  562.1 6.2 %reduce-scatter.5.cloned.1.call-done = f32[8,4,256]{2,0,1:T(8,128)} async-done(((f32[16,4,256]{2,0,1:T(8,128)}), f32[8,4,256]{2,0,1:T(8,128)}) %reduce-scatter.5.cloned.1.call-update) | async-done | bytes 32784 | tf_op jit(solution)/shard_map/reduce_scatter | solution.py:65
  (107 shorter events, 69.2 us)
Async XLA Ops:
  12.6 36.4 %collective-permute-start = (bf16[96,4096]{1,0:T(8,128)(2,1)}, bf16[96,4096]{1,0:T(8,128)(2,1)}, u32[]{:S(2)}, u32[]{:S(2)}) collective-permute-start(bf16[96,4096]{1,0:T(8,128)(2,1)} %bitcast.19), channel_id=1, source_target_pairs={{0,1},{1,2},{2,3},{3,4},{4,5},{5,6},{6,7},{7,8},{8,9},{9,10},{10,1... | collective-permute-start | bytes 2359304 | tf_op jit(solution)/shard_map/ppermute | solution.py:18
  43.0 262.9 %all-to-all-start = ((bf16[96,16,1024]{2,0,1:T(8,128)(2,1)}), bf16[96,16,1024]{2,0,1:T(8,128)(2,1)S(1)}, u32[]{:S(2)}, u32[]{:S(2)}) async-start(bf16[96,16,1024]{2,0,1:T(8,128)(2,1)} %copy.31), calls=%async_computation | async-start | bytes 6291456 | tf_op jit(solution)/shard_map/all_to_all | solution.py:51
  49.0 330.0 %all-gather.2.cloned.1.call-start = ((), (), s32[]{:S(2)}) async-start(), calls=%async_computation.3 | async-start | bytes 9437184 | tf_op jit(solution)/shard_map/all_gather | solution.py:52
  49.0 74.5 %collective-permute-start.1 = (bf16[96,4096]{1,0:T(8,128)(2,1)}, bf16[96,4096]{1,0:T(8,128)(2,1)S(1)}, u32[]{:S(2)}, u32[]{:S(2)}) collective-permute-start(bf16[96,4096]{1,0:T(8,128)(2,1)} %collective-permute-done), channel_id=1, source_target_pairs={{0,1},{1,2},{2,3},{3,4},{4,5},{5,6},{6,7},{7,8},{8,9},{9,10},{10,1... | collective-permute-start | bytes 2359304 | tf_op jit(solution)/shard_map/ppermute | solution.py:18
  51.0 75.3 %collective-permute-start.8 = (bf16[96,4096]{1,0:T(8,128)(2,1)}, bf16[96,4096]{1,0:T(8,128)(2,1)S(1)}, u32[]{:S(2)}, u32[]{:S(2)}) collective-permute-start(bf16[96,4096]{1,0:T(8,128)(2,1)} %bitcast.19), channel_id=1, source_target_pairs={{0,15},{1,0},{2,1},{3,2},{4,3},{5,4},{6,5},{7,6},{8,7},{9,8},{10,9... | collective-permute-start | bytes 2359304 | tf_op jit(solution)/shard_map/ppermute | solution.py:21
  123.5 32.6 %collective-permute-start.2 = (bf16[96,4096]{1,0:T(8,128)(2,1)S(1)}, bf16[96,4096]{1,0:T(8,128)(2,1)S(1)}, u32[]{:S(2)}, u32[]{:S(2)}) collective-permute-start(bf16[96,4096]{1,0:T(8,128)(2,1)S(1)} %collective-permute-done.1), channel_id=1, source_target_pairs={{0,1},{1,2},{2,3},{3,4},{4,5},{5,6},{6,7},{7,8},{8,9},{9,10},{10,1... | collective-permute-start | bytes 2359304 | tf_op jit(solution)/shard_map/ppermute | solution.py:18
  127.2 32.1 %collective-permute-start.9 = (bf16[96,4096]{1,0:T(8,128)(2,1)S(1)}, bf16[96,4096]{1,0:T(8,128)(2,1)S(1)}, u32[]{:S(2)}, u32[]{:S(2)}) collective-permute-start(bf16[96,4096]{1,0:T(8,128)(2,1)S(1)} %collective-permute-done.8), channel_id=1, source_target_pairs={{0,15},{1,0},{2,1},{3,2},{4,3},{5,4},{6,5},{7,6},{8,7},{9,8},{10,9... | collective-permute-start | bytes 2359304 | tf_op jit(solution)/shard_map/ppermute | solution.py:21
  156.1 21.0 %collective-permute-start.3 = (bf16[96,4096]{1,0:T(8,128)(2,1)S(1)}, bf16[96,4096]{1,0:T(8,128)(2,1)S(1)}, u32[]{:S(2)}, u32[]{:S(2)}) collective-permute-start(bf16[96,4096]{1,0:T(8,128)(2,1)S(1)} %collective-permute-done.2), channel_id=1, source_target_pairs={{0,1},{1,2},{2,3},{3,4},{4,5},{5,6},{6,7},{7,8},{8,9},{9,10},{10,1... | collective-permute-start | bytes 2359304 | tf_op jit(solution)/shard_map/ppermute | solution.py:18
  159.4 32.7 %collective-permute-start.10 = (bf16[96,4096]{1,0:T(8,128)(2,1)S(1)}, bf16[96,4096]{1,0:T(8,128)(2,1)S(1)}, u32[]{:S(2)}, u32[]{:S(2)}) collective-permute-start(bf16[96,4096]{1,0:T(8,128)(2,1)S(1)} %collective-permute-done.9), channel_id=1, source_target_pairs={{0,15},{1,0},{2,1},{3,2},{4,3},{5,4},{6,5},{7,6},{8,7},{9,8},{10,9... | collective-permute-start | bytes 2359304 | tf_op jit(solution)/shard_map/ppermute | solution.py:21
  177.1 93.8 %copy-start.15 = (bf16[96,4096]{1,0:T(8,128)(2,1)}, bf16[96,4096]{1,0:T(8,128)(2,1)S(1)}, u32[]{:S(2)}) copy-start(bf16[96,4096]{1,0:T(8,128)(2,1)S(1)} %collective-permute-done.3) | copy-start | bytes 2359300
  177.1 20.1 %collective-permute-start.4 = (bf16[96,4096]{1,0:T(8,128)(2,1)S(1)}, bf16[96,4096]{1,0:T(8,128)(2,1)S(1)}, u32[]{:S(2)}, u32[]{:S(2)}) collective-permute-start(bf16[96,4096]{1,0:T(8,128)(2,1)S(1)} %collective-permute-done.3), channel_id=1, source_target_pairs={{0,1},{1,2},{2,3},{3,4},{4,5},{5,6},{6,7},{7,8},{8,9},{9,10},{10,1... | collective-permute-start | bytes 2359304 | tf_op jit(solution)/shard_map/ppermute | solution.py:18
  192.1 43.0 %collective-permute-start.11 = (bf16[96,4096]{1,0:T(8,128)(2,1)S(1)}, bf16[96,4096]{1,0:T(8,128)(2,1)S(1)}, u32[]{:S(2)}, u32[]{:S(2)}) collective-permute-start(bf16[96,4096]{1,0:T(8,128)(2,1)S(1)} %collective-permute-done.10), channel_id=1, source_target_pairs={{0,15},{1,0},{2,1},{3,2},{4,3},{5,4},{6,5},{7,6},{8,7},{9,8},{10,9... | collective-permute-start | bytes 2359304 | tf_op jit(solution)/shard_map/ppermute | solution.py:21
  197.2 73.7 %copy-start.17 = (bf16[96,4096]{1,0:T(8,128)(2,1)}, bf16[96,4096]{1,0:T(8,128)(2,1)S(1)}, u32[]{:S(2)}) copy-start(bf16[96,4096]{1,0:T(8,128)(2,1)S(1)} %collective-permute-done.4) | copy-start | bytes 2359300
  197.2 54.6 %collective-permute-start.5 = (bf16[96,4096]{1,0:T(8,128)(2,1)S(1)}, bf16[96,4096]{1,0:T(8,128)(2,1)S(1)}, u32[]{:S(2)}, u32[]{:S(2)}) collective-permute-start(bf16[96,4096]{1,0:T(8,128)(2,1)S(1)} %collective-permute-done.4), channel_id=1, source_target_pairs={{0,1},{1,2},{2,3},{3,4},{4,5},{5,6},{6,7},{7,8},{8,9},{9,10},{10,1... | collective-permute-start | bytes 2359304 | tf_op jit(solution)/shard_map/ppermute | solution.py:18
  235.9 35.0 %collective-permute-start.12 = (bf16[96,4096]{1,0:T(8,128)(2,1)S(1)}, bf16[96,4096]{1,0:T(8,128)(2,1)}, u32[]{:S(2)}, u32[]{:S(2)}) collective-permute-start(bf16[96,4096]{1,0:T(8,128)(2,1)S(1)} %collective-permute-done.11), channel_id=1, source_target_pairs={{0,15},{1,0},{2,1},{3,2},{4,3},{5,4},{6,5},{7,6},{8,7},{9,8},{10,9... | collective-permute-start | bytes 2359304 | tf_op jit(solution)/shard_map/ppermute | solution.py:21
  251.7 19.2 %collective-permute-start.6 = (bf16[96,4096]{1,0:T(8,128)(2,1)S(1)}, bf16[96,4096]{1,0:T(8,128)(2,1)}, u32[]{:S(2)}, u32[]{:S(2)}) collective-permute-start(bf16[96,4096]{1,0:T(8,128)(2,1)S(1)} %collective-permute-done.5), channel_id=1, source_target_pairs={{0,1},{1,2},{2,3},{3,4},{4,5},{5,6},{6,7},{7,8},{8,9},{9,10},{10,1... | collective-permute-start | bytes 2359304 | tf_op jit(solution)/shard_map/ppermute | solution.py:18
  270.9 34.9 %collective-permute-start.13 = (bf16[96,4096]{1,0:T(8,128)(2,1)}, bf16[96,4096]{1,0:T(8,128)(2,1)}, u32[]{:S(2)}, u32[]{:S(2)}) collective-permute-start(bf16[96,4096]{1,0:T(8,128)(2,1)} %collective-permute-done.12), channel_id=1, source_target_pairs={{0,15},{1,0},{2,1},{3,2},{4,3},{5,4},{6,5},{7,6},{8,7},{9,8},{10,9... | collective-permute-start | bytes 2359304 | tf_op jit(solution)/shard_map/ppermute | solution.py:21
  271.0 51.1 %collective-permute-start.7 = (bf16[96,4096]{1,0:T(8,128)(2,1)}, bf16[96,4096]{1,0:T(8,128)(2,1)}, u32[]{:S(2)}, u32[]{:S(2)}) collective-permute-start(bf16[96,4096]{1,0:T(8,128)(2,1)} %collective-permute-done.6), channel_id=1, source_target_pairs={{0,1},{1,2},{2,3},{3,4},{4,5},{5,6},{6,7},{7,8},{8,9},{9,10},{10,1... | collective-permute-start | bytes 2359304 | tf_op jit(solution)/shard_map/ppermute | solution.py:18
  305.9 47.8 %collective-permute-start.14 = (bf16[96,4096]{1,0:T(8,128)(2,1)}, bf16[96,4096]{1,0:T(8,128)(2,1)}, u32[]{:S(2)}, u32[]{:S(2)}) collective-permute-start(bf16[96,4096]{1,0:T(8,128)(2,1)} %collective-permute-done.13), channel_id=1, source_target_pairs={{0,15},{1,0},{2,1},{3,2},{4,3},{5,4},{6,5},{7,6},{8,7},{9,8},{10,9... | collective-permute-start | bytes 2359304 | tf_op jit(solution)/shard_map/ppermute | solution.py:21
  307.6 55.2 %copy-start.10 = (bf16[96,4096]{1,0:T(8,128)(2,1)S(1)}, bf16[96,4096]{1,0:T(8,128)(2,1)}, u32[]{:S(2)}) copy-start(bf16[96,4096]{1,0:T(8,128)(2,1)} %copy-done.9) | copy-start | bytes 2359300
  307.6 56.2 %copy-start.6 = (bf16[96,4096]{1,0:T(8,128)(2,1)S(1)}, bf16[96,4096]{1,0:T(8,128)(2,1)}, u32[]{:S(2)}) copy-start(bf16[96,4096]{1,0:T(8,128)(2,1)} %copy-done.5) | copy-start | bytes 2359300
  307.6 61.3 %copy-start.4 = (bf16[96,4096]{1,0:T(8,128)(2,1)S(1)}, bf16[96,4096]{1,0:T(8,128)(2,1)}, u32[]{:S(2)}) copy-start(bf16[96,4096]{1,0:T(8,128)(2,1)} %copy-done.3) | copy-start | bytes 2359300
  307.6 62.2 %copy-start.8 = (bf16[96,4096]{1,0:T(8,128)(2,1)S(1)}, bf16[96,4096]{1,0:T(8,128)(2,1)}, u32[]{:S(2)}) copy-start(bf16[96,4096]{1,0:T(8,128)(2,1)} %copy-done.7) | copy-start | bytes 2359300
  307.6 254.4 %reduce-scatter.3.cloned.1.call-start = ((), (), s32[]{:S(2)}) async-start(), calls=%async_computation.4 | async-start | bytes 1114112 | tf_op jit(solution)/shard_map/reduce_scatter | solution.py:64
  307.8 53.0 %copy-start.18 = (bf16[96,4096]{1,0:T(8,128)(2,1)S(1)}, bf16[96,4096]{1,0:T(8,128)(2,1)}, u32[]{:S(2)}) copy-start(bf16[96,4096]{1,0:T(8,128)(2,1)} %copy-done.17) | copy-start | bytes 2359300
  307.8 54.0 %copy-start.16 = (bf16[96,4096]{1,0:T(8,128)(2,1)S(1)}, bf16[96,4096]{1,0:T(8,128)(2,1)}, u32[]{:S(2)}) copy-start(bf16[96,4096]{1,0:T(8,128)(2,1)} %copy-done.15) | copy-start | bytes 2359300
  307.9 62.9 %copy-start.12 = (bf16[96,4096]{1,0:T(8,128)(2,1)S(1)}, bf16[96,4096]{1,0:T(8,128)(2,1)}, u32[]{:S(2)}) copy-start(bf16[96,4096]{1,0:T(8,128)(2,1)} %copy-done.11) | copy-start | bytes 2359300
  307.9 63.9 %copy-start.14 = (bf16[96,4096]{1,0:T(8,128)(2,1)S(1)}, bf16[96,4096]{1,0:T(8,128)(2,1)}, u32[]{:S(2)}) copy-start(bf16[96,4096]{1,0:T(8,128)(2,1)} %copy-done.13) | copy-start | bytes 2359300
  441.0 128.8 %copy-start.1 = (f32[96,16,512]{2,1,0:T(8,128)S(1)}, f32[96,16,512]{2,1,0:T(8,128)}, u32[]{:S(2)}) copy-start(f32[96,16,512]{2,1,0:T(8,128)} %param.11) | copy-start | bytes 9437188
  452.5 109.4 %copy-start.22 = (f32[4]{0:T(128)S(1)}, f32[4]{0:T(128)}, u32[]{:S(2)}) copy-start(f32[4]{0:T(128)} %param.16) | copy-start | bytes 52
  452.6 109.4 %copy-start.23 = (f32[8]{0:T(128)S(1)}, f32[8]{0:T(128)}, u32[]{:S(2)}) copy-start(f32[8]{0:T(128)} %param.15) | copy-start | bytes 100
  459.3 108.9 %reduce-scatter.5.cloned.1.call-start = ((), (), s32[]{:S(2)}) async-start(), calls=%async_computation.5 | async-start | bytes 98304 | tf_op jit(solution)/shard_map/reduce_scatter | solution.py:65
  (12 other events, 170.2 us)
Sparse Core Ops, SparseCore 0:
  307.7 43.3 all-gather.1
  459.5 102.4 reduce-scatter.2
  564.1 4.0 reduce-scatter.4
